TPU v7x, 512 devices: a whole 4x4x16 slice. The times are simulated.
512 devices in a mesh: samp: 32 (over y_hi, z), head: 16 (over y_lo, x, core).
Axes of the slice: x: 4, y: 4 (y_hi: 2, y_lo: 2; y = y_hi * 2 + y_lo), z: 16, core: 2. Of those that a mesh axis runs over, the one named last changes fastest.
Arguments:
- queries: bfloat16 [32, 768, 512], P('samp', 'head'), may hold values from -10 to 10
- keys: bfloat16 [32, 768, 512], P('samp', 'head'), may hold values from -10 to 10
- values: bfloat16 [32, 768, 512], P('samp', 'head'), may hold values from -6 to 6
- out_grad: bfloat16 [32, 768, 512], P('samp', 'head'), may hold values from -6 to 6
- pair: bfloat16 [512, 512, 128], P('head', 'samp'), may hold values from -6 to 6
- ln_gain: float32 [128], replicated, may hold values from 0.25 to 1.75
- proj_weight: bfloat16 [128, 16], replicated, may hold values from -0.5 to 0.5
- token_mask: int32 [512], replicated, may hold values from 0 to 1, as said below
- atom_map: int32 [4096], replicated, may hold values from 0 to 511, never falling along the last dimension, each value on 1 to 24 neighbouring positions
Outputs:
- attended: bfloat16 [32, 768, 512], P('samp', 'head')
- query_grad: bfloat16 [32, 768, 512], P('samp', 'head')
- key_grad: bfloat16 [32, 768, 512], P('samp', 'head')
- value_grad: bfloat16 [32, 768, 512], P('samp', 'head')
- pair_grad: bfloat16 [512, 512, 128], P('head', 'samp')
- weight_grad: float32 [128, 16], replicated
- gain_grad: float32 [128], replicated
Inputs may be any that keep to these rules, and one draw needn't show every extreme that they name: `token_mask`: real tokens form a prefix of 256 or more tokens; the last token is padding.
All inputs are finite; a program needn't handle non-finite values.
Results may differ from a plain program's by a relative error of at most 0.02.
Values may be sent and summed in bfloat16 or wider, within the bound.
A program may use at most 64 MiB of HBM per device.

v0:
```python
import jax
import jax.numpy as jnp
from jax import lax
from jax.sharding import PartitionSpec as P


def token_weights(atom_map, token_mask):
    count = token_mask.shape[0]
    ends = jnp.searchsorted(atom_map, jnp.arange(count, dtype=jnp.int32), side="right")
    starts = jnp.concatenate([jnp.zeros((1,), jnp.int32), ends[:-1]])
    return (
        (ends - starts).astype(jnp.float32)
        * (count / atom_map.shape[0])
        * token_mask.astype(jnp.float32)
    )


def attend(query_row, key_row, value_row, grad_row, bias, key_keep, tok_weight):
    count = query_row.shape[1]
    local_heads = bias.shape[0]
    query_h = query_row.reshape(local_heads, -1, count)
    key_h = key_row.reshape(local_heads, -1, count)
    value_h = value_row.reshape(local_heads, -1, count)
    inv_root = 1.0 / jnp.sqrt(jnp.float32(query_h.shape[1]))
    scores = jnp.einsum(
        "hdi,hdj->hij", query_h, key_h, preferred_element_type=jnp.float32
    ) * inv_root + bias.astype(jnp.float32)
    scores = jnp.where(key_keep[None, None, :], scores, jnp.float32(-1000000000.0))
    largest = jnp.max(scores, axis=-1, keepdims=True)
    expo = jnp.exp(scores - largest)
    prob = expo / jnp.sum(expo, axis=-1, keepdims=True)
    prob_b = prob.astype(jnp.bfloat16)
    attended = jnp.einsum(
        "hij,hdj->hdi", prob_b, value_h, preferred_element_type=jnp.float32
    ).astype(jnp.bfloat16)
    grad_in = (grad_row.astype(jnp.float32) * tok_weight[None, :]).astype(jnp.bfloat16)
    grad_h = grad_in.reshape(local_heads, -1, count)
    dprob = jnp.einsum("hdi,hdj->hij", grad_h, value_h, preferred_element_type=jnp.float32)
    row_dot = jnp.sum(prob * dprob, axis=-1, keepdims=True)
    dscore = prob * (dprob - row_dot)
    dscore_b = dscore.astype(jnp.bfloat16)
    query_grad = (
        jnp.einsum("hij,hdj->hdi", dscore_b, key_h, preferred_element_type=jnp.float32) * inv_root
    ).astype(jnp.bfloat16)
    key_grad = (
        jnp.einsum("hij,hdi->hdj", dscore_b, query_h, preferred_element_type=jnp.float32) * inv_root
    ).astype(jnp.bfloat16)
    value_grad = jnp.einsum(
        "hij,hdi->hdj", prob_b, grad_h, preferred_element_type=jnp.float32
    ).astype(jnp.bfloat16)
    shape = (-1, count)
    return (
        attended.reshape(shape),
        query_grad.reshape(shape),
        key_grad.reshape(shape),
        value_grad.reshape(shape),
        dscore,
    )


def local(queries, keys, values, out_grad, pair, ln_gain, proj_weight, token_mask, atom_map):
    count = queries.shape[2]
    key_keep = token_mask > 0
    tok_weight = token_weights(atom_map, token_mask)
    wide = pair.astype(jnp.float32)
    center = jnp.mean(wide, axis=-1, keepdims=True)
    spread = jnp.mean(jnp.square(wide - center), axis=-1, keepdims=True)
    inv_std = 1.0 / jnp.sqrt(spread + 1e-05)
    normed = (wide - center) * inv_std
    lnout = (normed * ln_gain).astype(jnp.bfloat16)
    tile_bias = jnp.einsum(
        "ijc,ch->hij", lnout, proj_weight, preferred_element_type=jnp.float32
    ).astype(jnp.bfloat16)
    wide_rows = lax.all_gather(tile_bias, "samp", axis=2, tiled=True)
    bias = lax.all_to_all(wide_rows, "head", split_axis=0, concat_axis=1, tiled=True)

    def one_sample(total, items):
        query_row, key_row, value_row, grad_row = items
        attended, query_grad, key_grad, value_grad, dscore = attend(
            query_row, key_row, value_row, grad_row, bias, key_keep, tok_weight
        )
        return (total + dscore, (attended, query_grad, key_grad, value_grad))

    start = jnp.zeros(bias.shape, jnp.float32)
    bias_partial, outs = lax.scan(one_sample, start, (queries, keys, values, out_grad))
    attended, query_grad, key_grad, value_grad = outs
    summed = lax.psum_scatter(
        bias_partial.astype(jnp.bfloat16), "samp", scatter_dimension=2, tiled=True
    ).astype(jnp.float32)
    bias_grad = lax.all_to_all(
        summed.astype(jnp.bfloat16), "head", split_axis=1, concat_axis=0, tiled=True
    ).astype(summed.dtype)
    highest = lax.Precision.HIGHEST
    lnout_grad = jnp.einsum(
        "hij,ch->ijc", bias_grad, proj_weight.astype(jnp.float32), precision=highest
    )
    weight_part = jnp.einsum("ijc,hij->ch", lnout.astype(jnp.float32), bias_grad, precision=highest)
    gain_part = jnp.sum(lnout_grad * normed, axis=(0, 1))
    weight_sum, gain_sum = lax.psum((weight_part, gain_part), ("samp", "head"))
    scaled = lnout_grad * ln_gain
    pair_grad = (
        scaled
        - jnp.mean(scaled, axis=-1, keepdims=True)
        - normed * jnp.mean(scaled * normed, axis=-1, keepdims=True)
    ) * inv_std
    return (
        attended,
        query_grad,
        key_grad,
        value_grad,
        pair_grad.astype(jnp.bfloat16),
        weight_sum / count,
        gain_sum / count,
    )


def solution(mesh):
    placed = (
        P("samp", "head", None),
        P("samp", "head", None),
        P("samp", "head", None),
        P("samp", "head", None),
        P("head", "samp", None),
        P(),
        P(),
        P(),
        P(),
    )
    return jax.shard_map(
        local,
        mesh=mesh,
        in_specs=placed,
        out_specs=(
            P("samp", "head", None),
            P("samp", "head", None),
            P("samp", "head", None),
            P("samp", "head", None),
            P("head", "samp", None),
            P(),
            P(),
        ),
        check_vma=False,
    )
```

profile of v0, /device:TPU:1, one launch (start us, length us, event | category | flops | bytes accessed | tf_op | source)
XLA Modules:
  0.0 939.2 jit_solution(5410960035745740067)
XLA Ops:
  7.2 0.0 copy-start
  7.2 1.1 convert_reduce_fusion
  8.3 1.1 fusion.25
  9.4 1.2 fusion.4
  10.7 0.0 copy-start.1
  10.7 104.2 %all_gather.3 = bf16[16,32,512]{0,2,1:T(8,128)(2,1)} all-gather(bf16[16,32,16]{0,2,1:T(8,128)(2,1)S(1)} %fusion.4), channel_id=1, replica_groups=mesh['samp'=32,'head'=16] {'samp'}, dimensions={2}, use_global_device_ids=true | all-gather | bytes 540672 | tf_op jit(solution)/shard_map/all_gather | solution.py:74
  114.9 4.6 copy.27
  119.5 17.6 %all-to-all-start = ((bf16[16,32,512]{2,1,0:T(8,128)(2,1)}), bf16[16,32,512]{2,1,0:T(8,128)(2,1)S(1)}, u32[]{:S(2)}, u32[]{:S(2)}) async-start(bf16[16,32,512]{2,1,0:T(8,128)(2,1)} %copy.27), calls=%async_computation | async-start | bytes 1048576 | tf_op jit(solution)/shard_map/all_to_all | solution.py:75
  137.1 0.0 reduce-scatter.2.cloned.1.call-start
  137.1 0.0 copy-done.1
  137.2 0.0 copy-start.5
  137.2 0.0 copy-start.4
  137.2 42.1 %while.32 = (s32[]{:T(128)}, u32[512]{0:T(512)S(1)}, u32[512]{0:T(512)S(1)}, s32[4096]{0:T(1024)S(1)}, s32[]{:T(128)}, /*index=5*/s32[]{:T(128)}, s32[]{}) while((s32[]{:T(128)}, u32[512]{0:T(512)S(1)}, u32[512]{0:T(512)S(1)}, s32[4096]{0:T(1024)S(1)}, s32[]{:T(128)}, /*index=5*/s32[]{:T(128)}, s32[]{}) %tuple.50), condition=%wide.region_5.6_spmd.clone, body=%wide.region_4.5_spmd.clone.sunk | while | flops 10244 | bytes 37989 | solution.py:9
  137.2 3.1 gather_fusion
  140.5 3.1 gather_fusion
  143.7 3.1 gather_fusion
  146.9 3.1 gather_fusion
  150.2 3.1 gather_fusion
  153.4 3.1 gather_fusion
  156.6 3.1 gather_fusion
  159.9 3.1 gather_fusion
  163.1 3.1 gather_fusion
  166.4 3.1 gather_fusion
  169.6 3.1 gather_fusion
  172.8 3.1 gather_fusion
  176.1 3.1 gather_fusion
  179.3 0.0 copy-start.7
  179.3 0.0 copy-start.8
  179.3 0.0 copy-done.5
  179.3 0.1 fusion.51
  179.4 0.0 all-to-all-done
  179.4 0.1 bitcast_convert_fusion
  179.6 0.3 copy.28
  179.9 0.0 copy-done
  179.9 0.4 fusion.54
  180.3 0.2 fusion.12
  180.5 0.0 copy-done.8
  180.5 0.4 multiply_reduce_fusion
  180.9 1.1 multiply_convert_fusion
  182.0 0.0 reduce-scatter.2.cloned.1.call-update
  182.0 1.9 fusion.7
  183.9 0.9 fusion.10
  184.8 0.9 fusion.9
  185.7 616.3 %reduce-scatter.2.cloned.1.call-done = bf16[1,512,16]{1,2,0:T(8,128)(2,1)} async-done(((bf16[1,512,512]{1,2,0:T(8,128)(2,1)}), bf16[1,512,16]{1,2,0:T(8,128)(2,1)}) %reduce-scatter.2.cloned.1.call-update) | async-done | bytes 16400 | tf_op jit(solution)/shard_map/reduce_scatter | solution.py:87
  802.0 0.9 copy.29
  802.9 0.5 broadcast.127
  803.4 1.4 reduce.6
  804.9 0.8 reshape.193
  805.6 16.4 %all-to-all-start.1 = ((bf16[16,2,256]{2,1,0:T(2,128)(2,1)}), bf16[16,2,256]{2,1,0:T(2,128)(2,1)S(1)}, u32[]{:S(2)}, u32[]{:S(2)}) async-start(bf16[16,2,256]{2,1,0:T(2,128)(2,1)} %reshape.193), calls=%async_computation.2 | async-start | bytes 32768 | tf_op jit(solution)/shard_map/all_to_all | solution.py:90
  822.0 0.9 fusion.8
  822.9 4.9 all-to-all-done.1
  827.8 0.2 reshape.194
  828.0 0.1 copy.30
  828.1 0.1 all_to_all.8
  828.2 0.2 copy.32
  828.4 0.0 copy-done.3
  828.4 0.0 copy-done.6
  828.4 0.0 copy-done.9
  828.4 0.4 fusion.24
  828.9 0.3 convolution_bitcast_fusion
  829.2 101.0 %all-reduce = (f32[128,16]{0,1:T(8,128)S(1)}, f32[128]{0:T(128)S(1)}) all-reduce(f32[128,16]{0,1:T(8,128)S(1)} %convolution_bitcast_fusion, f32[128]{0:T(128)S(1)} %get-tuple-element.129), channel_id=1, replica_groups=mesh['samp'=32,'head'=16] {'samp','head'}, use_global_device_ids=true, to_apply=%region_10.11 | all-reduce | flops 2176 | bytes 17408 | tf_op jit(solution)/shard_map/psum | solution.py:99
  930.2 0.6 broadcast_multiply_fusion.3
  930.8 0.5 broadcast_multiply_fusion.4
  931.3 1.0 fusion.23
  (79 shorter events, 0.6 us)
Async XLA Ops:
  7.2 172.8 %copy-start = (bf16[1,48,512]{2,1,0:T(8,128)(2,1)S(1)}, bf16[1,48,512]{2,1,0:T(8,128)(2,1)}, u32[]{:S(2)}) copy-start(bf16[1,48,512]{2,1,0:T(8,128)(2,1)} %param.12) | copy-start | bytes 147460
  10.7 126.5 %copy-start.1 = (s32[4096]{0:T(1024)S(1)}, s32[4096]{0:T(1024)}, u32[]{:S(2)}) copy-start(s32[4096]{0:T(1024)} %param.19) | copy-start | bytes 49156
  119.5 59.9 %all-to-all-start = ((bf16[16,32,512]{2,1,0:T(8,128)(2,1)}), bf16[16,32,512]{2,1,0:T(8,128)(2,1)S(1)}, u32[]{:S(2)}, u32[]{:S(2)}) async-start(bf16[16,32,512]{2,1,0:T(8,128)(2,1)} %copy.27), calls=%async_computation | async-start | bytes 1048576 | tf_op jit(solution)/shard_map/all_to_all | solution.py:75
  137.1 664.9 %reduce-scatter.2.cloned.1.call-start = ((), (), s32[]{:S(2)}) async-start(), calls=%async_computation.3 | async-start | bytes 540672 | tf_op jit(solution)/shard_map/reduce_scatter | solution.py:87
  137.2 42.2 %copy-start.5 = (s32[512]{0:T(512)S(1)}, s32[512]{0:T(512)}, u32[]{:S(2)}) copy-start(s32[512]{0:T(512)} %param.18) | copy-start | bytes 6148
  137.2 42.8 %copy-start.4 = (bf16[1,48,512]{2,1,0:T(8,128)(2,1)S(1)}, bf16[1,48,512]{2,1,0:T(8,128)(2,1)}, u32[]{:S(2)}) copy-start(bf16[1,48,512]{2,1,0:T(8,128)(2,1)} %param.11) | copy-start | bytes 147460
  179.3 1.2 copy-start.7
  179.3 1.2 copy-start.8
  183.9 638.1 %copy-start.2 = (bf16[512,512]{0,1:T(8,128)(2,1)S(1)}, bf16[512,512]{0,1:T(8,128)(2,1)}, u32[]{:S(2)}) copy-start(bf16[512,512]{0,1:T(8,128)(2,1)} %multiply_convert_fusion) | copy-start | bytes 1572868
  184.8 643.6 %copy-start.3 = (bf16[32,16,128]{2,1,0:T(8,128)(2,1)S(1)}, bf16[32,16,128]{2,1,0:T(8,128)(2,1)}, u32[]{:S(2)}) copy-start(bf16[32,16,128]{2,1,0:T(8,128)(2,1)} %param.15) | copy-start | bytes 393220
  184.8 643.6 %copy-start.6 = (f32[128]{0:T(128)S(1)}, f32[128]{0:T(128)}, u32[]{:S(2)}) copy-start(f32[128]{0:T(128)} %param.16) | copy-start | bytes 1540
  184.8 643.6 %copy-start.9 = (bf16[128,16]{0,1:T(8,128)(2,1)S(1)}, bf16[128,16]{0,1:T(8,128)(2,1)}, u32[]{:S(2)}) copy-start(bf16[128,16]{0,1:T(8,128)(2,1)} %param.17) | copy-start | bytes 12292
  805.6 22.2 %all-to-all-start.1 = ((bf16[16,2,256]{2,1,0:T(2,128)(2,1)}), bf16[16,2,256]{2,1,0:T(2,128)(2,1)S(1)}, u32[]{:S(2)}, u32[]{:S(2)}) async-start(bf16[16,2,256]{2,1,0:T(2,128)(2,1)} %reshape.193), calls=%async_computation.2 | async-start | bytes 32768 | tf_op jit(solution)/shard_map/all_to_all | solution.py:90
Sparse Core Ops, SparseCore 0:
  182.1 619.8 reduce-scatter.1
where the time goes:
time: 940 us; the launch traced here: 939 us
  waiting for transfers between devices  621 us (66%)
  blocking collectives  205 us (22%)
  local copies, waits for them, and re-layouts  48.6 us (5%)
  starting transfers between devices  34 us (4%)
  between operations  14.3 us (2%)
    reduce_scatter x1, waiting for transfers between devices, local(): lax.psum_scatter(bias_partial.astype(jnp.bfloat16), 'samp', scatter_dimen...  616 us
    all_gather x1, blocking collectives, local(): wide_rows = lax.all_gather(tile_bias, 'samp', axis=2, tiled=True)  104 us
    psum x1, blocking collectives, local(): weight_sum, gain_sum = lax.psum((weight_part, gain_part), ('samp', 'head'))  101 us
    gather x13, local copies, waits for them, and re-layouts, token_weights(): jnp.searchsorted(atom_map, jnp.arange(count, dtype=jnp.int32), side='right')  40.9 us
  transfers between devices with their start and end apart: 3, of which 2 were waited for; matrix products, arithmetic and copies ran while one was open for 5% of the time, Pallas kernels for 0%

commit v1 on v0

--- a/solution.py
+++ b/solution.py
@@ -71,7 +71,9 @@
     tile_bias = jnp.einsum(
         "ijc,ch->hij", lnout, proj_weight, preferred_element_type=jnp.float32
     ).astype(jnp.bfloat16)
-    wide_rows = lax.all_gather(tile_bias, "samp", axis=2, tiled=True)
+    wide_rows = jnp.concatenate(
+        lax.all_to_all(jnp.stack([tile_bias] * lax.axis_size("samp")), "samp", 0, 0), axis=2
+    )
     bias = lax.all_to_all(wide_rows, "head", split_axis=0, concat_axis=1, tiled=True)
 
     def one_sample(total, items):

time: 940 us -> 880 us (0.936)
  blocking collectives: 205 us -> 101 us
  waiting for transfers between devices: 621 us -> 656 us
    all_gather x1 -> x0, blocking collectives: 104 us -> none  [local(): wide_rows = lax.all_gather(tile_bias, 'samp', axis=2, tiled=True)]
    all_to_all x0 -> x1, waiting for transfers between devices: none -> 32.1 us  [local(): lax.all_to_all(jnp.stack([tile_bias] * lax.axis_size('samp')), 'samp', 0, 0)]
    all_to_all x0 -> x1, starting transfers between devices: none -> 18.6 us  [local(): lax.all_to_all(jnp.stack([tile_bias] * lax.axis_size('samp')), 'samp', 0, 0)]
    all_to_all x1, starting transfers between devices: 17.6 us -> 5.91 us  [local(): lax.all_to_all(wide_rows, 'head', split_axis=0, concat_axis=1, tiled=True)]
  transfers between devices with their start and end apart: 3 -> 4, of which waited for: 2 -> 3; matrix products, arithmetic and copies ran while one was open for 5% -> 5% of each run, Pallas kernels for 0% -> 0%
where the time goes in v1:
time: 880 us; the launch traced here: 879 us
  waiting for transfers between devices  656 us (75%)
  blocking collectives  101 us (11%)
  local copies, waits for them, and re-layouts  51.2 us (6%)
  starting transfers between devices  40.9 us (5%)
  between operations  14.3 us (2%)
    reduce_scatter x1, waiting for transfers between devices, local(): lax.psum_scatter(bias_partial.astype(jnp.bfloat16), 'samp', scatter_dimen...  619 us
    psum x1, blocking collectives, local(): weight_sum, gain_sum = lax.psum((weight_part, gain_part), ('samp', 'head'))  101 us
    gather x13, local copies, waits for them, and re-layouts, token_weights(): jnp.searchsorted(atom_map, jnp.arange(count, dtype=jnp.int32), side='right')  40.9 us
    all_to_all x1, waiting for transfers between devices, local(): lax.all_to_all(jnp.stack([tile_bias] * lax.axis_size('samp')), 'samp', 0, 0)  32.1 us
    all_to_all x1, starting transfers between devices, local(): lax.all_to_all(jnp.stack([tile_bias] * lax.axis_size('samp')), 'samp', 0, 0)  18.6 us
  transfers between devices with their start and end apart: 4, of which 3 were waited for; matrix products, arithmetic and copies ran while one was open for 5% of the time, Pallas kernels for 0%

profile of v1, /device:TPU:1, one launch (start us, length us, event | category | flops | bytes accessed | tf_op | source)
XLA Modules:
  0.0 879.4 jit_solution(7339745270536019750)
XLA Ops:
  7.2 0.0 copy-start
  7.2 1.1 convert_reduce_fusion
  8.3 1.1 fusion.25
  9.4 1.2 fusion.4
  10.7 0.2 copy.34
  10.9 0.5 broadcast_bitcast_fusion
  11.3 2.7 reshape.203
  14.1 18.6 %all-to-all-start = ((bf16[32,2,4096]{2,1,0:T(2,128)(2,1)}), bf16[32,2,4096]{2,1,0:T(2,128)(2,1)S(1)}, u32[]{:S(2)}, u32[]{:S(2)}) async-start(bf16[32,2,4096]{2,1,0:T(2,128)(2,1)} %reshape.203), calls=%async_computation | async-start | bytes 1048576 | tf_op jit(solution)/shard_map/all_to_all | solution.py:75
  32.7 32.1 %all-to-all-done = bf16[32,2,4096]{2,1,0:T(2,128)(2,1)S(1)} async-done(((bf16[32,2,4096]{2,1,0:T(2,128)(2,1)}), bf16[32,2,4096]{2,1,0:T(2,128)(2,1)S(1)}, u32[]{:S(2)}, u32[]{:S(2)}) %all-to-all-start) | async-done | bytes 524320 | tf_op jit(solution)/shard_map/all_to_all | solution.py:75
  64.9 1.0 reshape.204
  65.9 0.4 bitcast_bitcast_fusion
  66.3 0.5 copy.35
  66.8 0.0 copy-start.1
  66.8 1.5 copy.36
  68.3 5.9 all-to-all-start.1
  74.2 0.0 reduce-scatter.2.cloned.1.call-start
  74.3 0.0 copy-start.5
  74.3 42.1 %while.32 = (s32[]{:T(128)}, u32[512]{0:T(512)S(1)}, u32[512]{0:T(512)S(1)}, s32[4096]{0:T(1024)S(1)}, s32[]{:T(128)}, /*index=5*/s32[]{:T(128)}, s32[]{}) while((s32[]{:T(128)}, u32[512]{0:T(512)S(1)}, u32[512]{0:T(512)S(1)}, s32[4096]{0:T(1024)S(1)}, s32[]{:T(128)}, /*index=5*/s32[]{:T(128)}, s32[]{}) %tuple.50), condition=%wide.region_5.6_spmd.clone, body=%wide.region_4.5_spmd.clone.sunk | while | flops 10244 | bytes 37989 | solution.py:9
  74.3 3.1 gather_fusion
  77.6 3.1 gather_fusion
  80.8 3.1 gather_fusion
  84.1 3.1 gather_fusion
  87.3 3.1 gather_fusion
  90.5 3.1 gather_fusion
  93.8 3.1 gather_fusion
  97.0 3.1 gather_fusion
  100.3 3.1 gather_fusion
  103.5 3.1 gather_fusion
  106.7 3.1 gather_fusion
  110.0 3.1 gather_fusion
  113.2 3.1 gather_fusion
  116.4 0.0 copy-start.4
  116.5 0.1 fusion.51
  116.5 0.2 bitcast_convert_fusion
  116.7 0.3 copy.37
  117.1 0.2 copy-done.4
  117.2 0.4 fusion.54
  117.6 0.2 fusion.12
  117.8 0.2 copy-done.7
  118.0 0.0 copy-done.8
  118.0 0.4 multiply_reduce_fusion
  118.4 1.1 multiply_convert_fusion
  119.5 0.0 reduce-scatter.2.cloned.1.call-update
  119.5 1.9 fusion.7
  121.4 0.9 fusion.10
  122.3 0.9 fusion.9
  123.2 619.0 %reduce-scatter.2.cloned.1.call-done = bf16[1,512,16]{1,2,0:T(8,128)(2,1)} async-done(((bf16[1,512,512]{1,2,0:T(8,128)(2,1)}), bf16[1,512,16]{1,2,0:T(8,128)(2,1)}) %reduce-scatter.2.cloned.1.call-update) | async-done | bytes 16400 | tf_op jit(solution)/shard_map/reduce_scatter | solution.py:89
  742.2 0.9 copy.38
  743.1 0.5 broadcast.129
  743.6 1.5 reduce.6
  745.1 0.8 reshape.205
  745.9 16.3 %all-to-all-start.2 = ((bf16[16,2,256]{2,1,0:T(2,128)(2,1)}), bf16[16,2,256]{2,1,0:T(2,128)(2,1)S(1)}, u32[]{:S(2)}, u32[]{:S(2)}) async-start(bf16[16,2,256]{2,1,0:T(2,128)(2,1)} %reshape.205), calls=%async_computation.3 | async-start | bytes 32768 | tf_op jit(solution)/shard_map/all_to_all | solution.py:92
  762.2 0.9 fusion.8
  763.1 4.9 all-to-all-done.2
  768.0 0.2 reshape.206
  768.2 0.1 copy.39
  768.3 0.1 all_to_all.22
  768.4 0.2 copy.41
  768.6 0.4 fusion.24
  769.1 0.3 convolution_bitcast_fusion
  769.4 101.1 %all-reduce = (f32[128,16]{0,1:T(8,128)S(1)}, f32[128]{0:T(128)S(1)}) all-reduce(f32[128,16]{0,1:T(8,128)S(1)} %convolution_bitcast_fusion, f32[128]{0:T(128)S(1)} %get-tuple-element.129), channel_id=1, replica_groups=mesh['samp'=32,'head'=16] {'samp','head'}, use_global_device_ids=true, to_apply=%region_10.11 | all-reduce | flops 2176 | bytes 17408 | tf_op jit(solution)/shard_map/psum | solution.py:101
  870.5 0.6 broadcast_multiply_fusion.3
  871.1 0.5 broadcast_multiply_fusion.4
  871.6 1.0 fusion.23
  (86 shorter events, 0.6 us)
Async XLA Ops:
  7.2 109.9 %copy-start = (bf16[1,48,512]{2,1,0:T(8,128)(2,1)S(1)}, bf16[1,48,512]{2,1,0:T(8,128)(2,1)}, u32[]{:S(2)}) copy-start(bf16[1,48,512]{2,1,0:T(8,128)(2,1)} %param.12) | copy-start | bytes 147460
  14.1 50.8 %all-to-all-start = ((bf16[32,2,4096]{2,1,0:T(2,128)(2,1)}), bf16[32,2,4096]{2,1,0:T(2,128)(2,1)S(1)}, u32[]{:S(2)}, u32[]{:S(2)}) async-start(bf16[32,2,4096]{2,1,0:T(2,128)(2,1)} %reshape.203), calls=%async_computation | async-start | bytes 1048576 | tf_op jit(solution)/shard_map/all_to_all | solution.py:75
  66.8 7.5 copy-start.1
  68.3 48.2 %all-to-all-start.1 = ((bf16[16,32,512]{2,1,0:T(8,128)(2,1)}), bf16[16,32,512]{2,1,0:T(8,128)(2,1)S(1)}, u32[]{:S(2)}, u32[]{:S(2)}) async-start(bf16[16,32,512]{2,1,0:T(8,128)(2,1)} %copy.36), calls=%async_computation.1 | async-start | bytes 1048576 | tf_op jit(solution)/shard_map/all_to_all | solution.py:77
  74.2 668.0 %reduce-scatter.2.cloned.1.call-start = ((), (), s32[]{:S(2)}) async-start(), calls=%async_computation.4 | async-start | bytes 540672 | tf_op jit(solution)/shard_map/reduce_scatter | solution.py:89
  74.3 42.1 %copy-start.5 = (s32[512]{0:T(512)S(1)}, s32[512]{0:T(512)}, u32[]{:S(2)}) copy-start(s32[512]{0:T(512)} %param.18) | copy-start | bytes 6148
  116.4 0.8 copy-start.4
  117.2 0.8 copy-start.7
  117.2 0.8 copy-start.8
  122.3 639.9 %copy-start.2 = (bf16[512,512]{0,1:T(8,128)(2,1)S(1)}, bf16[512,512]{0,1:T(8,128)(2,1)}, u32[]{:S(2)}) copy-start(bf16[512,512]{0,1:T(8,128)(2,1)} %multiply_convert_fusion) | copy-start | bytes 1572868
  123.2 645.4 %copy-start.3 = (bf16[32,16,128]{2,1,0:T(8,128)(2,1)S(1)}, bf16[32,16,128]{2,1,0:T(8,128)(2,1)}, u32[]{:S(2)}) copy-start(bf16[32,16,128]{2,1,0:T(8,128)(2,1)} %param.15) | copy-start | bytes 393220
  123.2 645.4 %copy-start.6 = (f32[128]{0:T(128)S(1)}, f32[128]{0:T(128)}, u32[]{:S(2)}) copy-start(f32[128]{0:T(128)} %param.16) | copy-start | bytes 1540
  123.2 645.4 %copy-start.9 = (bf16[128,16]{0,1:T(8,128)(2,1)S(1)}, bf16[128,16]{0,1:T(8,128)(2,1)}, u32[]{:S(2)}) copy-start(bf16[128,16]{0,1:T(8,128)(2,1)} %param.17) | copy-start | bytes 12292
  745.9 22.1 %all-to-all-start.2 = ((bf16[16,2,256]{2,1,0:T(2,128)(2,1)}), bf16[16,2,256]{2,1,0:T(2,128)(2,1)S(1)}, u32[]{:S(2)}, u32[]{:S(2)}) async-start(bf16[16,2,256]{2,1,0:T(2,128)(2,1)} %reshape.205), calls=%async_computation.3 | async-start | bytes 32768 | tf_op jit(solution)/shard_map/all_to_all | solution.py:92
Sparse Core Ops, SparseCore 0:
  119.6 622.5 reduce-scatter.1
